TPU v7x, 128 devices: a whole 4x4x4 slice. The times are simulated.
128 devices in a mesh: dom: 16 (over z, x), band: 8 (over y, core).
Axes of the slice: x: 4, y: 4, z: 4, core: 2. Of those that a mesh axis runs over, the one named last changes fastest.
Arguments:
- orbitals: float32 [2560, 32, 8, 128], P('band', 'dom'), may hold values from -12 to 12, as said below
- potential: float32 [32, 8, 128], P('dom'), may hold values from -2 to 0
Outputs:
- filtered: float32 [2560, 32, 8, 128], P('band', 'dom')
Inputs may be any that keep to these rules, and one draw needn't show every extreme that they name: real-valued orbitals.
All inputs are finite; a program needn't handle non-finite values.
Results may differ from a plain program's by a relative error of at most 0.00029.
Values sent between devices are 32-bit elements; how exact they have to be, the bound alone decides.
A program may use at most 192 MiB of HBM per device.

v0:
```python
import jax
import jax.numpy as jnp
from jax import lax
from jax.sharding import PartitionSpec as P

PANEL = 64
PANELS = 3
NS_ITERS = 16


SHIFT = 1.0
HALF = 1.5


def with_halo(shard, sides, width):
    for axis, dim in sides:
        size, length = (lax.axis_size(axis), shard.shape[dim])
        up = [(i, (i + 1) % size) for i in range(size)]
        down = [(j, i) for i, j in up]
        last = lax.slice_in_dim(shard, length - width, length, axis=dim)
        initial = lax.slice_in_dim(shard, 0, width, axis=dim)
        before = lax.ppermute(last, axis, up)
        after = lax.ppermute(initial, axis, down)
        shard = jnp.concatenate([before, shard, after], axis=dim)
    return shard


def from_root(block, axis, source):
    block = jnp.where(lax.axis_index(axis) == source, block, jnp.zeros_like(block))
    return lax.psum(block, axis)


def hdot(left, right):
    return jnp.dot(left, right, precision=lax.Precision.HIGHEST, preferred_element_type=jnp.float32)


def rolled(values, offset, which):
    return jnp.roll(values, offset, axis=which)


def apply_h(field_pad, potential_pad):
    centre = field_pad[:, 1:-1]
    upper = field_pad[:, 2:]
    lower = field_pad[:, :-2]
    face_sum = (
        upper
        + lower
        + rolled(centre, 1, 2)
        + rolled(centre, -1, 2)
        + rolled(centre, 1, 3)
        + rolled(centre, -1, 3)
    )
    edge_sum = jnp.zeros_like(centre)
    for offset in (1, -1):
        edge_sum = (
            edge_sum
            + rolled(upper, offset, 2)
            + rolled(lower, offset, 2)
            + rolled(upper, offset, 3)
            + rolled(lower, offset, 3)
        )
        for second in (1, -1):
            edge_sum = edge_sum + rolled(rolled(centre, offset, 2), second, 3)
    laplace = (2.0 * face_sum + edge_sum - 24.0 * centre) / 6.0
    weighted = potential_pad[None] * field_pad
    middle = weighted[:, 1:-1]
    near_sum = (
        weighted[:, 2:]
        + weighted[:, :-2]
        + rolled(middle, 1, 2)
        + rolled(middle, -1, 2)
        + rolled(middle, 1, 3)
        + rolled(middle, -1, 3)
    )
    return -0.5 * laplace + 0.5 * middle + near_sum / 12.0


def inv_sqrt(correlation):
    order = correlation.shape[0]
    eye = jnp.eye(order, dtype=jnp.float32)
    scale = jnp.sqrt(jnp.sum(correlation * correlation))
    root = correlation / scale
    inverse = eye
    for turn in range(NS_ITERS):
        factor = 0.5 * (3.0 * eye - hdot(inverse, root))
        root = hdot(root, factor)
        inverse = hdot(factor, inverse)
    return inverse / jnp.sqrt(scale)


def sweep_rim(field):
    return with_halo(field, (("dom", 1),), 1)


def per_device(orbitals, potential):
    count = orbitals.shape[0]
    potential_pad = with_halo(potential, (("dom", 0),), 1)
    first = (apply_h(sweep_rim(orbitals), potential_pad) - SHIFT * orbitals) / HALF
    second = 2.0 * (apply_h(sweep_rim(first), potential_pad) - SHIFT * first) / HALF - orbitals
    shape = second.shape
    rows = second.reshape(count, -1)
    band = lax.axis_index("band")
    local_row = jnp.arange(count)
    for panel_index in range(PANELS):
        panel = rows[:PANEL]
        correlation = lax.psum(hdot(panel, panel.T), "dom")
        outgoing = hdot(inv_sqrt(correlation), panel)
        basis = from_root(outgoing, "band", panel_index)
        coeffs = lax.psum(hdot(basis, rows.T), "dom")
        keep = jnp.where((local_row < PANEL) & (band <= panel_index), 0.0, 1.0).astype(jnp.float32)
        rows = rows - keep[:, None] * hdot(coeffs.T, basis)
        rows = rows.at[:PANEL].set(jnp.where(band == panel_index, basis, rows[:PANEL]))
    return rows.reshape(shape)


def solution(mesh):
    in_specs = (P("band", "dom", None, None), P("dom", None, None))
    out_specs = P("band", "dom", None, None)
    return jax.shard_map(
        per_device, mesh=mesh, in_specs=in_specs, out_specs=out_specs, check_vma=False
    )
```

profile of v0, /device:TPU:16, one launch (start us, length us, event | category | flops | bytes accessed | tf_op | source)
XLA Modules:
  0.0 932.4 jit_solution(11688201332727117582)
XLA Ops:
  9.3 6.3 collective-permute-start
  15.7 5.5 collective-permute-start.3
  21.8 3.6 fusion.177
  25.4 4.9 fusion.11
  33.6 4.9 fusion.12
  38.5 10.7 %collective-permute-done.2 = f32[1,8,128]{2,1,0:T(8,128)S(1)} collective-permute-done((f32[1,8,128]{2,1,0:T(8,128)S(1)}, f32[1,8,128]{2,1,0:T(8,128)S(1)}, u32[]{:S(2)}, u32[]{:S(2)}) %collective-permute-start.2) | collective-permute-done | bytes 4128 | tf_op jit(solution)/shard_map/ppermute | solution.py:22
  49.8 3.4 fusion.166
  53.2 3.3 fusion.167
  61.9 3.4 fusion.172
  65.3 3.3 fusion.173
  81.4 30.6 %broadcast_multiply_fusion = (f32[320,2,8,128]{3,0,2,1:T(8,128)S(1)}, f32[320,2,8,128]{3,0,2,1:T(8,128)}) fusion(f32[320,2,8,1]{3,0,2,1:T(8,128)} %get-tuple-element.60, f32[320,2,8,127]{3,0,2,1:T(8,128)} %get-tuple-element.62, f32[320,2,8,127]{3,0,2,1:T(8,128)} %get-tuple-element.61, f32[320,2,8,1]{3,0,2,1:T(8,128)} %get-tuple-element.59, ...), kind=kLoop, calls=%fused_computation.176 | loop fusion | flops 34078720 | bytes 73400320 | tf_op jit(solution)/shard_map/div | solution.py:98
  115.7 27.6 %collective-permute-done.4 = f32[320,1,8,128]{3,0,2,1:T(8,128)} collective-permute-done((f32[320,1,8,128]{3,0,2,1:T(8,128)}, f32[320,1,8,128]{3,0,2,1:T(8,128)}, u32[]{:S(2)}, u32[]{:S(2)}) %collective-permute-start.4) | collective-permute-done | bytes 1310752 | tf_op jit(solution)/shard_map/ppermute | solution.py:23
  143.3 3.6 collective-permute-done.5
  146.9 5.8 fusion.88
  180.6 6.6 fusion.46
  187.2 9.6 %fusion.43 = (f32[320,2,8,127]{3,0,2,1:T(8,128)}, f32[320,2,8,127]{3,0,2,1:T(8,128)}, f32[320,2,8,127]{3,0,2,1:T(8,128)}, f32[320,2,8,127]{3,0,2,1:T(8,128)}, f3...) fusion(f32[320,2,8,128]{3,0,2,1:T(8,128)S(1)} %get-tuple-element.45, f32[320,1,8,128]{3,0,2,1:T(8,128)} %collective-permute-done.5, ...), kind=kLoop, calls=%fused_computation.116 | loop fusion | flops 2600960 | bytes 26091520 | tf_op jit(solution)/shard_map/concatenate | solution.py:24
  196.7 30.3 %fusion.30 = f32[320,2,8,128]{3,0,2,1:T(8,128)} fusion(f32[320,2,8,128]{3,0,2,1:T(8,128)S(1)} %get-tuple-element.45, f32[320,2,1,128]{3,0,2,1:T(8,128)S(1)} %get-tuple-element.105, f32[320,2,7,128]{3,0,2,1:T(8,128)} %copy-done.3, f32[320,2,7,128]{3,0,2,1:T(8,128)} %copy-done.4, f32[320,2,1,128]{3,0,2,1:T(8,128)S(1)} %get-tuple-element.106, ...), kind=kLoop, calls=%fused_computation.103 | loop fusion | flops 37355520 | bytes 73359360 | tf_op jit(solution)/shard_map/sub | solution.py:99
  229.0 69.7 %psum.63 = f32[64,64]{1,0:T(8,128)S(1)} all-reduce(f32[64,64]{1,0:T(8,128)S(1)} %convolution_bitcast_fusion), channel_id=1, replica_groups=mesh['dom'=16,'band'=8] {'dom'}, use_global_device_ids=true, to_apply=%region_0.1 | all-reduce | flops 4096 | bytes 32768 | tf_op jit(solution)/shard_map/psum | solution.py:106
  313.2 49.9 %all-reduce.7.cloned.1.call-done = f32[64,2048]{1,0:T(8,128)} async-done(((f32[64,2048]{1,0:T(8,128)}), f32[64,2048]{1,0:T(8,128)}) %all-reduce.7.cloned.1.call-update) | async-done | bytes 524304 | tf_op jit(solution)/shard_map/psum | solution.py:30
  363.1 4.6 fusion.52
  368.0 85.3 %all-reduce.9.cloned.1.call-done = f32[64,320]{1,0:T(8,128)} async-done(((f32[64,320]{1,0:T(8,128)}), f32[64,320]{1,0:T(8,128)}) %all-reduce.9.cloned.1.call-update) | async-done | bytes 81936 | tf_op jit(solution)/shard_map/psum | solution.py:109
  453.3 4.8 fusion.2
  458.9 72.1 %psum.66 = f32[64,64]{1,0:T(8,128)S(1)} all-reduce(f32[64,64]{1,0:T(8,128)S(1)} %fusion.211), channel_id=1, replica_groups=mesh['dom'=16,'band'=8] {'dom'}, use_global_device_ids=true, to_apply=%region_4.5 | all-reduce | flops 4096 | bytes 32768 | tf_op jit(solution)/shard_map/psum | solution.py:106
  541.8 53.2 %all-reduce.11.cloned.1.call-done = f32[64,2048]{1,0:T(8,128)} async-done(((f32[64,2048]{1,0:T(8,128)}), f32[64,2048]{1,0:T(8,128)}) %all-reduce.11.cloned.1.call-update) | async-done | bytes 524304 | tf_op jit(solution)/shard_map/psum | solution.py:30
  594.9 4.2 fusion.240
  599.2 85.5 %all-reduce.13.cloned.1.call-done = f32[64,320]{1,0:T(8,128)} async-done(((f32[64,320]{1,0:T(8,128)}), f32[64,320]{1,0:T(8,128)}) %all-reduce.13.cloned.1.call-update) | async-done | bytes 81936 | tf_op jit(solution)/shard_map/psum | solution.py:109
  684.7 4.7 fusion.1
  691.9 72.4 %psum.69 = f32[64,64]{1,0:T(8,128)S(1)} all-reduce(f32[64,64]{1,0:T(8,128)S(1)} %fusion.241), channel_id=1, replica_groups=mesh['dom'=16,'band'=8] {'dom'}, use_global_device_ids=true, to_apply=%region_8.9 | all-reduce | flops 4096 | bytes 32768 | tf_op jit(solution)/shard_map/psum | solution.py:106
  775.1 53.2 %all-reduce.15.cloned.1.call-done = f32[64,2048]{1,0:T(8,128)} async-done(((f32[64,2048]{1,0:T(8,128)}), f32[64,2048]{1,0:T(8,128)}) %all-reduce.15.cloned.1.call-update) | async-done | bytes 524304 | tf_op jit(solution)/shard_map/psum | solution.py:30
  828.3 5.0 fusion.270
  833.4 85.6 %all-reduce.17.cloned.1.call-done = f32[64,320]{1,0:T(8,128)} async-done(((f32[64,320]{1,0:T(8,128)}), f32[64,320]{1,0:T(8,128)}) %all-reduce.17.cloned.1.call-update) | async-done | bytes 81936 | tf_op jit(solution)/shard_map/psum | solution.py:109
  919.0 4.2 fusion
  (236 shorter events, 97.2 us)
Async XLA Ops:
  6.5 356.6 %all-reduce.7.cloned.1.call-start = ((), (), s32[]{:S(2)}) async-start(), calls=%async_computation | async-start | bytes 1048576 | tf_op jit(solution)/shard_map/psum | solution.py:30
  9.1 6.5 copy-start.12
  9.3 40.0 %collective-permute-start = (f32[320,1,8,128]{3,0,2,1:T(8,128)S(1)}, f32[320,1,8,128]{3,0,2,1:T(8,128)S(1)}, u32[]{:S(2)}, u32[]{:S(2)}) collective-permute-start(f32[320,1,8,128]{3,0,2,1:T(8,128)S(1)} %get-tuple-element.136), channel_id=1, source_target_pairs={{8,0},{16,8},{24,16},{32,24},{40,32},{48,40},{56,48},{64,56},{72,6... | collective-permute-start | bytes 3932168 | tf_op jit(solution)/shard_map/ppermute | solution.py:23
  15.6 33.7 %collective-permute-start.1 = (f32[320,1,8,128]{3,0,2,1:T(8,128)S(1)}, f32[320,1,8,128]{3,0,2,1:T(8,128)S(1)}, u32[]{:S(2)}, u32[]{:S(2)}) collective-permute-start(f32[320,1,8,128]{3,0,2,1:T(8,128)S(1)} %get-tuple-element.135), channel_id=1, source_target_pairs={{0,8},{8,16},{16,24},{24,32},{32,40},{40,48},{48,56},{56,64},{64,7... | collective-permute-start | bytes 3932168 | tf_op jit(solution)/shard_map/ppermute | solution.py:22
  15.6 33.6 %collective-permute-start.2 = (f32[1,8,128]{2,1,0:T(8,128)S(1)}, f32[1,8,128]{2,1,0:T(8,128)S(1)}, u32[]{:S(2)}, u32[]{:S(2)}) collective-permute-start(f32[1,8,128]{2,1,0:T(8,128)S(1)} %get-tuple-element.137), channel_id=1, source_target_pairs={{0,8},{8,16},{16,24},{24,32},{32,40},{40,48},{48,56},{56,64},{64,7... | collective-permute-start | bytes 12296 | tf_op jit(solution)/shard_map/ppermute | solution.py:22
  15.7 33.6 %collective-permute-start.3 = (f32[1,8,128]{2,1,0:T(8,128)S(1)}, f32[1,8,128]{2,1,0:T(8,128)S(1)}, u32[]{:S(2)}, u32[]{:S(2)}) collective-permute-start(f32[1,8,128]{2,1,0:T(8,128)S(1)} %get-tuple-element.138), channel_id=1, source_target_pairs={{8,0},{16,8},{24,16},{32,24},{40,32},{48,40},{56,48},{64,56},{72,6... | collective-permute-start | bytes 12296 | tf_op jit(solution)/shard_map/ppermute | solution.py:23
  21.7 11.8 %copy-start.5 = (f32[320,2,7,128]{3,0,2,1:T(8,128)}, f32[320,2,7,128]{3,0,2,1:T(8,128)S(1)}, u32[]{:S(2)}) copy-start(f32[320,2,7,128]{3,0,2,1:T(8,128)S(1)} %get-tuple-element.127) | copy-start | bytes 6881284
  21.7 11.8 %copy-start.6 = (f32[320,2,7,128]{3,0,2,1:T(8,128)}, f32[320,2,7,128]{3,0,2,1:T(8,128)S(1)}, u32[]{:S(2)}) copy-start(f32[320,2,7,128]{3,0,2,1:T(8,128)S(1)} %get-tuple-element.128) | copy-start | bytes 6881284
  59.2 1.7 copy-start.1
  61.8 18.8 %copy-start = (f32[320,3,8,128]{3,0,2,1:T(8,128)}, f32[320,3,8,128]{3,0,2,1:T(8,128)S(1)}, u32[]{:S(2)}) copy-start(f32[320,3,8,128]{3,0,2,1:T(8,128)S(1)} %get-tuple-element.130) | copy-start | bytes 11796484
  113.7 29.6 %collective-permute-start.4 = (f32[320,1,8,128]{3,0,2,1:T(8,128)}, f32[320,1,8,128]{3,0,2,1:T(8,128)}, u32[]{:S(2)}, u32[]{:S(2)}) collective-permute-start(f32[320,1,8,128]{3,0,2,1:T(8,128)} %get-tuple-element.115), channel_id=1, source_target_pairs={{8,0},{16,8},{24,16},{32,24},{40,32},{48,40},{56,48},{64,56},{72,6... | collective-permute-start | bytes 3932168 | tf_op jit(solution)/shard_map/ppermute | solution.py:23
  113.9 33.0 %collective-permute-start.5 = (f32[320,1,8,128]{3,0,2,1:T(8,128)}, f32[320,1,8,128]{3,0,2,1:T(8,128)}, u32[]{:S(2)}, u32[]{:S(2)}) collective-permute-start(f32[320,1,8,128]{3,0,2,1:T(8,128)} %get-tuple-element.116), channel_id=1, source_target_pairs={{0,8},{8,16},{16,24},{24,32},{32,40},{40,48},{48,56},{56,64},{64,7... | collective-permute-start | bytes 3932168 | tf_op jit(solution)/shard_map/ppermute | solution.py:22
  152.7 6.3 copy-start.3
  152.7 12.7 %copy-start.4 = (f32[320,2,7,128]{3,0,2,1:T(8,128)}, f32[320,2,7,128]{3,0,2,1:T(8,128)S(1)}, u32[]{:S(2)}) copy-start(f32[320,2,7,128]{3,0,2,1:T(8,128)S(1)} %get-tuple-element.102) | copy-start | bytes 6881284
  187.2 9.6 %copy-start.2 = (f32[320,2,8,128]{3,2,1,0:T(8,128)S(1)}, f32[320,2,8,128]{3,2,1,0:T(8,128)}, u32[]{:S(2)}) copy-start(f32[320,2,8,128]{3,2,1,0:T(8,128)} %param.8) | copy-start | bytes 7864324
  300.3 7.3 slice-start
  309.9 143.5 %all-reduce.9.cloned.1.call-start = ((), (), s32[]{:S(2)}) async-start(), calls=%async_computation.1 | async-start | bytes 196608 | tf_op jit(solution)/shard_map/psum | solution.py:109
  313.2 54.8 %copy-start.7 = (f32[320,2,8,128]{3,2,1,0:T(8,128)}, f32[320,2,8,128]{3,2,1,0:T(8,128)S(1)}, u32[]{:S(2)}) copy-start(f32[320,2,8,128]{3,2,1,0:T(8,128)S(1)} %copy.35) | copy-start | bytes 7864324
  363.1 90.2 %copy-start.8 = (f32[64,2048]{1,0:T(8,128)S(1)}, f32[64,2048]{1,0:T(8,128)}, u32[]{:S(2)}) copy-start(f32[64,2048]{1,0:T(8,128)} %all-reduce.7.cloned.1.call-done) | copy-start | bytes 1572868
  367.7 227.2 %all-reduce.11.cloned.1.call-start = ((), (), s32[]{:S(2)}) async-start(), calls=%async_computation.2 | async-start | bytes 1048576 | tf_op jit(solution)/shard_map/psum | solution.py:30
  453.3 4.8 copy-start.9
  541.7 143.0 %all-reduce.13.cloned.1.call-start = ((), (), s32[]{:S(2)}) async-start(), calls=%async_computation.3 | async-start | bytes 196608 | tf_op jit(solution)/shard_map/psum | solution.py:109
  594.9 89.8 %copy-start.10 = (f32[64,2048]{1,0:T(8,128)S(1)}, f32[64,2048]{1,0:T(8,128)}, u32[]{:S(2)}) copy-start(f32[64,2048]{1,0:T(8,128)} %all-reduce.11.cloned.1.call-done) | copy-start | bytes 1572868
  599.1 229.2 %all-reduce.15.cloned.1.call-start = ((), (), s32[]{:S(2)}) async-start(), calls=%async_computation.4 | async-start | bytes 1048576 | tf_op jit(solution)/shard_map/psum | solution.py:30
  775.1 143.9 %all-reduce.17.cloned.1.call-start = ((), (), s32[]{:S(2)}) async-start(), calls=%async_computation.5 | async-start | bytes 196608 | tf_op jit(solution)/shard_map/psum | solution.py:109
  828.3 90.6 %copy-start.11 = (f32[64,2048]{1,0:T(8,128)S(1)}, f32[64,2048]{1,0:T(8,128)}, u32[]{:S(2)}) copy-start(f32[64,2048]{1,0:T(8,128)} %all-reduce.15.cloned.1.call-done) | copy-start | bytes 1572868
Sparse Core Ops, SparseCore 0:
  310.0 53.0 all-reduce.6
  367.9 85.4 all-reduce.8
  541.8 53.0 all-reduce.10
  599.2 85.4 all-reduce.12
  775.2 53.0 all-reduce.14
  833.5 85.4 all-reduce.16
where the time goes:
time: 936 us; the launch traced here: 932 us
  waiting for transfers between devices  455 us (49%)
  blocking collectives  214 us (23%)
  other arithmetic  115 us (12%)
  local copies, waits for them, and re-layouts  58.9 us (6%)
  matrix products  57.6 us (6%)
  between operations  17.3 us (2%)
  starting transfers between devices  14.3 us (2%)
    psum x3, waiting for transfers between devices, per_device(): coeffs = lax.psum(hdot(basis, rows.T), 'dom')  256 us
    psum x3, blocking collectives, per_device(): correlation = lax.psum(hdot(panel, panel.T), 'dom')  214 us
    psum x3, waiting for transfers between devices, from_root(): return lax.psum(block, axis)  156 us
    dot_general x153, matrix products, hdot(): jnp.dot(left, right, precision=lax.Precision.HIGHEST, preferred_element_t...  57.6 us
    slice x20, local copies, waits for them, and re-layouts, rolled(): return jnp.roll(values, offset, axis=which)  46.2 us
    div x1, other arithmetic, per_device(): (apply_h(sweep_rim(orbitals), potential_pad) - SHIFT * orbitals) / HALF  30.6 us
    sub x1, other arithmetic, per_device(): 2.0 * (apply_h(sweep_rim(first), potential_pad) - SHIFT * first) / HALF  30.3 us
    ppermute x3, waiting for transfers between devices, with_halo(): after = lax.ppermute(initial, axis, down)  27.6 us
  transfers between devices with their start and end apart: 12, of which 9 were waited for; matrix products, arithmetic and copies ran while one was open for 2% of the time, Pallas kernels for 0%

commit v1 on v0

v1 whole, which is shorter than its diff:
```python
import jax
import jax.numpy as jnp
from jax import lax
from jax.experimental import pallas as pl
from jax.experimental.pallas import tpu as pltpu
from jax.sharding import PartitionSpec as P

PANEL = 64
PANELS = 3
NS_ITERS = 16
ROWS = 320
DOM = 16
BAND = 8
ALL = PANEL * PANELS
CUTS = (0, 32, 64, 128, 192, 224, 256, 288, 320)
CHUNKS = tuple((a, b - a) for a, b in zip(CUTS, CUTS[1:]))
EARLY = 5
MESH = pl.DeviceIdType.MESH
F32 = jnp.float32
BF16 = jnp.bfloat16


def pieces(value, count):
    out = []
    for _ in range(count - 1):
        head = value.astype(BF16)
        out.append(head)
        value = value - head.astype(F32)
    out.append(value.astype(BF16))
    return out


def mm(left, right):
    return jnp.dot(left, right, preferred_element_type=F32)


def mm_t(left, right):
    return lax.dot_general(left, right, (((1,), (1,)), ((), ())), preferred_element_type=F32)


def exact(left, right):
    a0, a1, a2 = pieces(left, 3)
    b0, b1, b2 = pieces(right, 3)
    a = jnp.concatenate([a0, a0, a1, a0, a2, a1], axis=1)
    b = jnp.concatenate([b0, b1, b0, b2, b0, b1], axis=0)
    return mm(a, b)


def exact_in_two(left, right):
    a0, a1, a2 = pieces(left, 3)
    b0, b1, b2 = pieces(right, 3)
    large = mm(jnp.concatenate([a0, a0, a1], axis=1), jnp.concatenate([b0, b1, b0], axis=0))
    return large + mm(jnp.concatenate([a0, a2, a1], axis=1), jnp.concatenate([b2, b0, b1], axis=0))


def exact_t(left, right):
    a0, a1, a2 = pieces(left, 3)
    b0, b1, b2 = pieces(right, 3)
    a = jnp.concatenate([a0, a0, a1, a0, a2, a1], axis=1)
    b = jnp.concatenate([b0, b1, b0, b2, b0, b1], axis=1)
    return mm_t(a, b)


def identity(order):
    row = lax.broadcasted_iota(jnp.int32, (order, order), 0)
    return (row == lax.broadcasted_iota(jnp.int32, (order, order), 1)).astype(F32)


def inv_sqrt(correlation):
    eye = identity(PANEL)
    scale = jnp.sqrt(jnp.sum(correlation * correlation, keepdims=True))

    def turn(_, carry):
        root, inverse = carry
        factor = 0.5 * (3.0 * eye - exact_in_two(inverse, root))
        return exact_in_two(root, factor), exact_in_two(factor, inverse)

    _, inverse = lax.fori_loop(0, NS_ITERS, turn, (correlation / scale, eye))
    return inverse / jnp.sqrt(scale)


def around(value, axis):
    return pltpu.roll(value, 1, axis) + pltpu.roll(value, value.shape[axis] - 1, axis)


def twelve_h(field, weighted, j):
    v, w = field[j], weighted[j]
    outer = field[j - 1] + field[j + 1]
    part = w - 2.0 * v - outer
    near = weighted[j - 1] + weighted[j + 1]
    return 24.0 * v + 6.0 * w - 2.0 * outer + near + around(part, 0) + around(part - around(v, 0), 1)


def filtered(v, pot):
    w = [a * b for a, b in zip(v, pot)]
    first = [None] + [twelve_h(v, w, j) * (1.0 / 18.0) - v[j] * (2.0 / 3.0) for j in range(1, 5)] + [None]
    w = [None] + [first[j] * pot[j] for j in range(1, 5)] + [None]
    return [twelve_h(first, w, j) * (1.0 / 9.0) - first[j] * (4.0 / 3.0) - v[j] for j in (2, 3)]


class Sum:
    def __init__(self, refs, rows, dom):
        self.loc, self.zin, self.part, self.xin, self.full, self.send, self.recv = refs
        self.n = rows // 4
        self.z = dom // 4
        self.x = lax.rem(dom, 4)
        self.zs = [lax.rem(self.z + k, 4) for k in (1, 2, 3)]
        self.xs = [lax.rem(self.x + k, 4) for k in (1, 2, 3)]

    def block(self, ref, z):
        return ref.at[pl.ds(pl.multiple_of(z * self.n, 8), self.n)]

    def copies(self, phase):
        out = []
        for k in range(3):
            if phase == 0:
                src, dst = self.block(self.loc, self.zs[k]), self.zin.at[k]
            elif phase == 1:
                src, dst = self.part, self.xin.at[k]
            else:
                src = dst = self.block(self.full, self.z)
            to = self.z * 4 + self.xs[k] if phase == 1 else self.zs[k] * 4 + self.x
            out.append(
                pltpu.make_async_remote_copy(
                    src_ref=src,
                    dst_ref=dst,
                    send_sem=self.send.at[phase, k],
                    recv_sem=self.recv.at[phase, k],
                    device_id={"dom": to},
                    device_id_type=MESH,
                )
            )
        return out

    def start(self):
        for copy in self.copies(0):
            copy.start()

    def over_z(self):
        for copy in self.copies(0):
            copy.wait_recv()
        mine = self.block(self.loc, self.z)
        self.part[...] = mine[...] + self.zin[0] + self.zin[1] + self.zin[2]
        for copy in self.copies(1):
            copy.start()

    def over_x(self):
        for copy in self.copies(1):
            copy.wait_recv()
        mine = self.block(self.full, self.z)
        mine[...] = self.part[...] + self.xin[0] + self.xin[1] + self.xin[2]
        for copy in self.copies(2):
            copy.start()

    def end(self):
        for copy in self.copies(2):
            copy.wait_recv()

    def sent(self):
        for phase in range(3):
            for copy in self.copies(phase):
                copy.wait_send()


def sum_scratch(rows):
    n = rows // 4
    return [
        pltpu.VMEM((rows, ALL), F32),
        pltpu.VMEM((3, n, ALL), F32),
        pltpu.VMEM((n, ALL), F32),
        pltpu.VMEM((3, n, ALL), F32),
        pltpu.VMEM((rows, ALL), F32),
        pltpu.SemaphoreType.DMA((3, 3)),
        pltpu.SemaphoreType.DMA((3, 3)),
    ]


BULK = 256


def body(orb, pot, y_out, p_out, d_out, own, left_in, right_in, pots, ym, pm, ph, plo, *rest):
    sums, sems = rest[:21], rest[21:]
    halo_s, halo_r, pot_s, pot_r, pan_s, pan_r, relay_s, local = sems
    dom, band = lax.axis_index("dom"), lax.axis_index("band")
    core, y = lax.rem(band, 2), band // 2
    right, left = lax.rem(dom + 1, DOM), lax.rem(dom + DOM - 1, DOM)
    gram = Sum(sums[:7], ALL, dom)
    bulk = Sum(sums[7:14], BULK, dom)
    last = Sum(sums[14:], ROWS - BULK, dom)

    barrier = pltpu.get_barrier_semaphore()
    peers = [{"dom": right}, {"dom": left}]
    peers += [{"dom": z * 4 + gram.x} for z in gram.zs] + [{"dom": gram.z * 4 + x} for x in gram.xs]
    peers += [{"band": lax.rem(band + k, BAND)} for k in range(1, BAND)]
    for peer in peers:
        pl.semaphore_signal(barrier, inc=1, device_id=peer, device_id_type=MESH)
    pl.semaphore_wait(barrier, len(peers))

    def remote(src, dst, send, recv, device):
        return pltpu.make_async_remote_copy(
            src_ref=src, dst_ref=dst, send_sem=send, recv_sem=recv, device_id=device, device_id_type=MESH
        )

    def halo(c):
        rows = pl.ds(*CHUNKS[c])
        return [
            remote(orb.at[rows], left_in.at[rows], halo_s.at[0, c], halo_r.at[0, c], {"dom": right}),
            remote(orb.at[rows], right_in.at[rows], halo_s.at[1, c], halo_r.at[1, c], {"dom": left}),
        ]

    def pot_halo():
        return [
            remote(pot, pots.at[0], pot_s.at[0], pot_r.at[0], {"dom": right}),
            remote(pot, pots.at[2], pot_s.at[1], pot_r.at[1], {"dom": left}),
        ]

    for copy in pot_halo():
        copy.start()
    for c in range(EARLY):
        for copy in halo(c):
            copy.start()
    mine = [pltpu.make_async_copy(orb, own, local.at[0]), pltpu.make_async_copy(pot, pots.at[1], local.at[1])]
    for copy in mine:
        copy.start()
    for copy in mine:
        copy.wait()
    for copy in pot_halo():
        copy.wait_recv()

    flat = ym.reshape(16 * ROWS, 128)

    def run_filter(c):
        begin, count = CHUNKS[c]
        for copy in halo(c):
            copy.wait_recv()
        potential = [pots[j // 2, j % 2] for j in range(6)]

        def some(i, _):
            for step in range(2):
                o = begin + 2 * i + step
                v = [left_in[o, 0], left_in[o, 1], own[o, 0], own[o, 1], right_in[o, 0], right_in[o, 1]]
                for plane, value in enumerate(filtered(v, potential)):
                    flat[pl.ds(plane * 8 * ROWS + o, 8, stride=ROWS), :] = value
            return 0

        lax.fori_loop(0, count // 2, some, 0)

    def y_copy(c):
        rows = pl.ds(*CHUNKS[c])
        return pltpu.make_async_copy(ym.at[:, rows], y_out.at[:, rows], local.at[2 + c])

    def panel_rows(p, half):
        return pm.at[:, pl.ds(p * PANEL + half * 32, 32)]

    def owner_copies(p, half):
        rows = ym.at[:, pl.ds(half * 32, 32)]
        targets = [p ^ 1, (p + 2) % BAND, (p + 4) % BAND, (p + 6) % BAND]
        return [
            remote(rows, panel_rows(p, half), pan_s.at[half, k], pan_r.at[p, half], {"band": t})
            for k, t in enumerate(targets)
        ]

    def relay_copy(p, half):
        ref = panel_rows(p, half)
        return remote(ref, ref, relay_s.at[p, half], pan_r.at[p, half], {"band": band + 1 - 2 * core})

    def relays(p):
        return (core == p % 2) & (y != p // 2)

    def send_panel(half):
        for p in range(PANELS):

            @pl.when(band == p)
            def _():
                for copy in owner_copies(p, half):
                    copy.start()
                begin, count = CHUNKS[half]
                pm[:, p * PANEL + begin : p * PANEL + begin + count] = ym[:, begin : begin + count]

    def take_panel(half):
        for p in range(PANELS):

            @pl.when(band != p)
            def _():
                relay_copy(p, half).wait_recv()

            @pl.when(relays(p))
            def _():
                relay_copy(p, half).start()

    def inner(c, total, at):
        begin, count = CHUNKS[c]

        def some(k, acc):
            a0, a1 = pieces(ym[k, begin : begin + count], 2)
            b0, b1 = ph[k], plo[k]
            return acc + (mm_t(a0, b0) + (mm_t(a0, b1) + mm_t(a1, b0)))

        total.loc[at : at + count] = lax.fori_loop(0, 16, some, jnp.zeros((count, ALL), F32))

    run_filter(0)
    send_panel(0)
    run_filter(1)
    send_panel(1)
    take_panel(0)
    run_filter(2)
    y_copy(2).start()
    take_panel(1)

    p_copy = pltpu.make_async_copy(pm, p_out, local.at[2 + len(CHUNKS)])
    p_copy.start()

    def gram_step(k, acc):
        a0, a1 = pieces(pm[k], 2)
        ph[k] = a0
        plo[k] = a1
        return acc + (mm_t(a0, a0) + (mm_t(a0, a1) + mm_t(a1, a0)))

    gram.loc[...] = lax.fori_loop(0, 16, gram_step, jnp.zeros((ALL, ALL), F32))
    gram.start()
    inner(0, bulk, 0)
    inner(1, bulk, 32)
    inner(2, bulk, 64)
    gram.over_z()
    for c in range(EARLY, len(CHUNKS)):
        for copy in halo(c):
            copy.start()
    for half in range(2):
        for p in range(PANELS):

            @pl.when(band == p)
            def _():
                for copy in owner_copies(p, half):
                    copy.wait_send()
                begin, count = CHUNKS[half]
                ym[:, begin : begin + count] = jnp.zeros((16, count, 128), F32)

        y_copy(half).start()
    run_filter(3)
    y_copy(3).start()
    inner(3, bulk, 128)
    gram.over_x()
    run_filter(4)
    y_copy(4).start()
    inner(4, bulk, 192)
    gram.end()

    g = gram.full[...]
    eye = identity(PANEL)
    none = jnp.zeros((PANEL, PANEL), F32)
    t0 = jnp.concatenate([inv_sqrt(g[:PANEL, :PANEL]), none, none], axis=1)
    t0g = exact(t0, g)
    a = jnp.concatenate([jnp.concatenate([none, eye, none], axis=1), jnp.concatenate([none, none, eye], axis=1)], axis=0)
    a = a - exact(exact_t(g[PANEL:], t0), t0)
    ag = exact(a, g)
    s1 = exact_t(ag[:PANEL], a[:PANEL])
    run_filter(5)
    y_copy(5).start()
    inner(5, bulk, 224)
    bulk.start()
    t1 = exact(inv_sqrt(s1), a[:PANEL])
    t1g = exact(t1, g)
    a = a[PANEL:] - exact(exact_t(ag[PANEL:], t1), t1)
    s2 = exact_t(exact(a, g), a)
    bulk.over_z()
    run_filter(6)
    y_copy(6).start()
    inner(6, last, 0)
    run_filter(7)
    y_copy(7).start()
    inner(7, last, 32)
    last.start()
    t2 = exact(inv_sqrt(s2), a)
    bulk.over_x()
    last.over_z()
    t2g = exact(t2, g)
    r0 = t0
    r1 = t1 - exact(exact_t(t1g, t0), r0)
    r2 = t2 - exact(exact_t(t2g, t0), r0) - exact(exact_t(t2g, t1), r1)
    t = jnp.concatenate([t0, t1, t2], axis=0)
    r = jnp.concatenate([r0, r1, r2], axis=0)
    bulk.end()
    last.over_x()
    d_out[:BULK] = exact(exact_t(bulk.full[...], r), t)
    for p, rows in enumerate((t0, t1, t2)):

        @pl.when(band == p)
        def _():
            d_out[:PANEL] = -rows

    last.end()
    d_out[BULK:] = exact(exact_t(last.full[...], r), t)

    for c in range(len(CHUNKS)):
        for copy in halo(c):
            copy.wait_send()
        y_copy(c).wait()
    for copy in pot_halo():
        copy.wait_send()
    for half in range(2):
        for p in range(PANELS):

            @pl.when(relays(p))
            def _():
                relay_copy(p, half).wait_send()

    p_copy.wait()
    for total in (gram, bulk, last):
        total.sent()


def project(orb, pot):
    scratch = [pltpu.VMEM((ROWS, 2, 8, 128), F32)] * 3 + [
        pltpu.VMEM((3, 2, 8, 128), F32),
        pltpu.VMEM((16, ROWS, 128), F32),
        pltpu.VMEM((16, ALL, 128), F32),
        pltpu.VMEM((16, ALL, 128), BF16),
        pltpu.VMEM((16, ALL, 128), BF16),
    ]
    scratch += sum_scratch(ALL) + sum_scratch(BULK) + sum_scratch(ROWS - BULK)
    scratch += [
        pltpu.SemaphoreType.DMA((2, len(CHUNKS))),
        pltpu.SemaphoreType.DMA((2, len(CHUNKS))),
        pltpu.SemaphoreType.DMA((2,)),
        pltpu.SemaphoreType.DMA((2,)),
        pltpu.SemaphoreType.DMA((2, 4)),
        pltpu.SemaphoreType.DMA((PANELS, 2)),
        pltpu.SemaphoreType.DMA((PANELS, 2)),
        pltpu.SemaphoreType.DMA((3 + len(CHUNKS),)),
    ]
    anywhere = pl.BlockSpec(memory_space=pl.ANY)
    return pl.pallas_call(
        body,
        out_shape=(
            jax.ShapeDtypeStruct((16, ROWS, 128), F32),
            jax.ShapeDtypeStruct((16, ALL, 128), F32),
            jax.ShapeDtypeStruct((ROWS, ALL), F32),
        ),
        in_specs=[anywhere, anywhere],
        out_specs=(anywhere, anywhere, pl.BlockSpec(memory_space=pltpu.VMEM)),
        scratch_shapes=scratch,
        compiler_params=pltpu.CompilerParams(collective_id=0, has_side_effects=True, vmem_limit_bytes=40 << 20),
        name="filter_and_project",
    )(orb, pot)


STEP = 64


def update_body(y, p, d, out, ph, plo):
    @pl.when(pl.program_id(0) == 0)
    def _():
        def cast(k, _):
            ph[k], plo[k] = pieces(p[k], 2)
            return 0

        lax.fori_loop(0, 16, cast, 0)

    d0, d1 = pieces(d[...], 2)
    flat = out.reshape(STEP * 16, 128)

    def some(k, _):
        rows = y[k] - (mm(d0, ph[k]) + (mm(d0, plo[k]) + mm(d1, ph[k])))
        for i in range(STEP // 8):
            flat[pl.ds(i * 128 + k, 8, stride=16), :] = rows[i * 8 : i * 8 + 8]
        return 0

    lax.fori_loop(0, 16, some, 0)


def update(y, p, d):
    return pl.pallas_call(
        update_body,
        grid=(ROWS // STEP,),
        out_shape=jax.ShapeDtypeStruct((ROWS, 2, 8, 128), F32),
        in_specs=[
            pl.BlockSpec((16, STEP, 128), lambda i: (0, i, 0)),
            pl.BlockSpec((16, ALL, 128), lambda i: (0, 0, 0), pipeline_mode=pl.Buffered(1)),
            pl.BlockSpec((STEP, ALL), lambda i: (i, 0)),
        ],
        out_specs=pl.BlockSpec((STEP, 2, 8, 128), lambda i: (i, 0, 0, 0)),
        scratch_shapes=[pltpu.VMEM((16, ALL, 128), BF16), pltpu.VMEM((16, ALL, 128), BF16)],
        compiler_params=pltpu.CompilerParams(vmem_limit_bytes=24 << 20),
        name="apply_update",
    )(y, p, d)


def per_device(orbitals, potential):
    return update(*project(orbitals, potential))


def solution(mesh):
    spec = P("band", "dom", None, None)
    return jax.shard_map(
        per_device, mesh=mesh, in_specs=(spec, P("dom", None, None)), out_specs=spec, check_vma=False
    )
```

time: 936 us -> 159 us (0.17)
  waiting for transfers between devices: 455 us -> 0 us
  blocking collectives: 214 us -> 0 us
  Pallas kernels: 0 us -> 156 us
  other arithmetic: 115 us -> 0 us
  matrix products: 57.6 us -> 0 us
  local copies, waits for them, and re-layouts: 58.9 us -> 2.44 us
  between operations: 17.3 us -> 0.01 us
  starting transfers between devices: 14.3 us -> 0 us
    psum x6 -> x0, waiting for transfers between devices: 413 us -> none  [the longest x3 256 us: per_device(): coeffs = lax.psum(hdot(basis, rows.T), 'dom')]
    psum x3 -> x0, blocking collectives: 214 us -> none  [per_device(): correlation = lax.psum(hdot(panel, panel.T), 'dom')]
    pallas_call x0 -> x2, Pallas kernels: none -> 156 us  [the longest x1 139 us: project(): pl.pallas_call(body, out_shape=(jax.ShapeDtypeStruct((16, ROWS, 128), F32...]
    dot_general x153 -> x0, matrix products: 57.6 us -> none  [hdot(): jnp.dot(left, right, precision=lax.Precision.HIGHEST, preferred_element_t...]
    slice x26 -> x0, local copies, waits for them, and re-layouts: 48.4 us -> none  [the longest x20 46.2 us: rolled(): return jnp.roll(values, offset, axis=which)]
    concatenate x11 -> x0, other arithmetic: 47.6 us -> none  [the longest x5 24.9 us: with_halo(): shard = jnp.concatenate([before, shard, after], axis=dim)]
    ppermute x6 -> x0, waiting for transfers between devices: 42 us -> none  [the longest x3 27.6 us: with_halo(): after = lax.ppermute(initial, axis, down)]
    div x1 -> x0, other arithmetic: 30.6 us -> none  [per_device(): (apply_h(sweep_rim(orbitals), potential_pad) - SHIFT * orbitals) / HALF]
  transfers between devices with their start and end apart: 12 -> 0, of which waited for: 9 -> 0; matrix products, arithmetic and copies ran while one was open for 2% -> 0% of each run, Pallas kernels for 0% -> 0%
where the time goes in v1:
time: 159 us
  Pallas kernels  156 us (98%)
  local copies, waits for them, and re-layouts  2.44 us (2%)
    pallas_call x1, Pallas kernels, project(): pl.pallas_call(body, out_shape=(jax.ShapeDtypeStruct((16, ROWS, 128), F32...  139 us
    pallas_call x1, Pallas kernels, update(): pl.pallas_call(update_body, grid=(ROWS // STEP,), out_shape=jax.ShapeDtyp...  16.9 us

profile of v1, /device:TPU:16, one launch (start us, length us, event | category | flops | bytes accessed | tf_op | source)
XLA Modules:
  0.0 158.5 jit_solution(8761687798714113464)
XLA Ops:
  0.0 0.0 copy-start
  0.0 1.7 %copy-done = f32[320,2,8,128]{3,2,1,0:T(8,128)S(1)} copy-done((f32[320,2,8,128]{3,2,1,0:T(8,128)S(1)}, f32[320,2,8,128]{3,2,1,0:T(8,128)}, u32[]{:S(2)}) %copy-start) | copy-done | bytes 2621464
  1.7 0.0 copy-start.1
  1.7 0.7 copy-done.1
  2.4 139.2 %filter_and_project.1 = (f32[16,320,128]{2,1,0:T(8,128)S(1)}, f32[16,192,128]{2,1,0:T(8,128)S(1)}, f32[320,192]{1,0:T(8,128)S(1)}) custom-call(f32[320,2,8,128]{3,2,1,0:T(8,128)S(1)} %copy-done, f32[2,8,128]{2,1,0:T(8,128)S(1)} %copy-done.1), custom_call_target="tpu_custom_call" | custom-call | tf_op jit(solution)/shard_map/filter_and_project/pallas_call | solution.py:432
  141.7 16.9 %apply_update.1 = f32[320,2,8,128]{3,2,1,0:T(8,128)} custom-call(f32[16,320,128]{2,1,0:T(8,128)S(1)} %get-tuple-element.8.y, f32[16,192,128]{2,1,0:T(8,128)S(1)} %get-tuple-element.9.p, f32[320,192]{1,0:T(8,128)S(1)} %get-tuple-element.10.d), custom_call_target="tpu_custom_call" | custom-call | tf_op jit(solution)/shard_map/apply_update/pallas_call | solution.py:472
Async XLA Ops:
  0.0 1.7 %copy-start = (f32[320,2,8,128]{3,2,1,0:T(8,128)S(1)}, f32[320,2,8,128]{3,2,1,0:T(8,128)}, u32[]{:S(2)}) copy-start(f32[320,2,8,128]{3,2,1,0:T(8,128)} %orb.1) | copy-start | bytes 7864324
  1.7 0.7 copy-start.1

commit v2 on v1

--- a/solution.py
+++ b/solution.py
@@ -12,9 +12,10 @@
 DOM = 16
 BAND = 8
 ALL = PANEL * PANELS
-CUTS = (0, 32, 64, 128, 192, 224, 256, 288, 320)
+CUTS = (0, 32, 64, 128, 192, 208, 224, 240, 256, 320)
 CHUNKS = tuple((a, b - a) for a, b in zip(CUTS, CUTS[1:]))
-EARLY = 5
+EARLY = 4
+TOGETHER = 8
 MESH = pl.DeviceIdType.MESH
 F32 = jnp.float32
 BF16 = jnp.bfloat16
@@ -46,11 +47,14 @@
     return mm(a, b)
 
 
-def exact_in_two(left, right):
+def exact_twice(left, right):
     a0, a1, a2 = pieces(left, 3)
     b0, b1, b2 = pieces(right, 3)
-    large = mm(jnp.concatenate([a0, a0, a1], axis=1), jnp.concatenate([b0, b1, b0], axis=0))
-    return large + mm(jnp.concatenate([a0, a2, a1], axis=1), jnp.concatenate([b2, b0, b1], axis=0))
+    low = lax.broadcasted_iota(jnp.int32, left.shape, 1) < PANEL
+    a01 = jnp.where(low, left, left - a0.astype(F32)).astype(BF16)
+    a12 = jnp.where(low, a1.astype(F32), a2.astype(F32)).astype(BF16)
+    large = mm(jnp.concatenate([a0, a01], axis=1), jnp.concatenate([b0, b1, b2, b0], axis=0))
+    return large + mm(a12, jnp.concatenate([b1, b0], axis=0))
 
 
 def exact_t(left, right):
@@ -66,17 +70,24 @@
     return (row == lax.broadcasted_iota(jnp.int32, (order, order), 1)).astype(F32)
 
 
-def inv_sqrt(correlation):
-    eye = identity(PANEL)
+def inv_sqrt(correlation, between=()):
+    eye = jnp.concatenate([identity(PANEL), identity(PANEL)], axis=1)
+    twice = jnp.concatenate([correlation, correlation], axis=1)
     scale = jnp.sqrt(jnp.sum(correlation * correlation, keepdims=True))
 
     def turn(_, carry):
         root, inverse = carry
-        factor = 0.5 * (3.0 * eye - exact_in_two(inverse, root))
-        return exact_in_two(root, factor), exact_in_two(factor, inverse)
-
-    _, inverse = lax.fori_loop(0, NS_ITERS, turn, (correlation / scale, eye))
-    return inverse / jnp.sqrt(scale)
+        factor = 0.5 * (3.0 * eye - exact_twice(inverse, root))
+        return exact_twice(root, factor), exact_twice(factor, inverse)
+
+    carry = (twice / scale, eye)
+    parts = len(between) + 1
+    for part in range(parts):
+        turns = NS_ITERS * (part + 1) // parts - NS_ITERS * part // parts
+        carry = lax.fori_loop(0, turns, turn, carry)
+        if part < len(between):
+            between[part]()
+    return (carry[1] / jnp.sqrt(scale))[:, :PANEL]
 
 
 def around(value, axis):
@@ -208,6 +219,10 @@
             remote(orb.at[rows], right_in.at[rows], halo_s.at[1, c], halo_r.at[1, c], {"dom": left}),
         ]
 
+    def send_halo(c):
+        for copy in halo(c):
+            copy.start()
+
     def pot_halo():
         return [
             remote(pot, pots.at[0], pot_s.at[0], pot_r.at[0], {"dom": right}),
@@ -217,8 +232,7 @@
     for copy in pot_halo():
         copy.start()
     for c in range(EARLY):
-        for copy in halo(c):
-            copy.start()
+        send_halo(c)
     mine = [pltpu.make_async_copy(orb, own, local.at[0]), pltpu.make_async_copy(pot, pots.at[1], local.at[1])]
     for copy in mine:
         copy.start()
@@ -236,14 +250,14 @@
         potential = [pots[j // 2, j % 2] for j in range(6)]
 
         def some(i, _):
-            for step in range(2):
-                o = begin + 2 * i + step
+            for step in range(TOGETHER):
+                o = begin + TOGETHER * i + step
                 v = [left_in[o, 0], left_in[o, 1], own[o, 0], own[o, 1], right_in[o, 0], right_in[o, 1]]
                 for plane, value in enumerate(filtered(v, potential)):
                     flat[pl.ds(plane * 8 * ROWS + o, 8, stride=ROWS), :] = value
             return 0
 
-        lax.fori_loop(0, count // 2, some, 0)
+        lax.fori_loop(0, count // TOGETHER, some, 0)
 
     def y_copy(c):
         rows = pl.ds(*CHUNKS[c])
@@ -288,15 +302,14 @@
             def _():
                 relay_copy(p, half).start()
 
-    def inner(c, total, at):
-        begin, count = CHUNKS[c]
-
+    def inner(begin, count, total, at):
         def some(k, acc):
             a0, a1 = pieces(ym[k, begin : begin + count], 2)
             b0, b1 = ph[k], plo[k]
-            return acc + (mm_t(a0, b0) + (mm_t(a0, b1) + mm_t(a1, b0)))
-
-        total.loc[at : at + count] = lax.fori_loop(0, 16, some, jnp.zeros((count, ALL), F32))
+            both = mm_t(jnp.concatenate([a0, a1], axis=1), jnp.concatenate([b0, b0], axis=1))
+            return acc + (both + mm_t(a0, b1))
+
+        total.loc[at : at + count] = lax.fori_loop(0, 16, some, jnp.zeros((count, ALL), F32), unroll=4)
 
     run_filter(0)
     send_panel(0)
@@ -316,15 +329,12 @@
         plo[k] = a1
         return acc + (mm_t(a0, a0) + (mm_t(a0, a1) + mm_t(a1, a0)))
 
-    gram.loc[...] = lax.fori_loop(0, 16, gram_step, jnp.zeros((ALL, ALL), F32))
+    gram.loc[...] = lax.fori_loop(0, 16, gram_step, jnp.zeros((ALL, ALL), F32), unroll=4)
     gram.start()
-    inner(0, bulk, 0)
-    inner(1, bulk, 32)
-    inner(2, bulk, 64)
+    send_halo(4)
+    inner(0, 128, bulk, 0)
     gram.over_z()
-    for c in range(EARLY, len(CHUNKS)):
-        for copy in halo(c):
-            copy.start()
+    send_halo(5)
     for half in range(2):
         for p in range(PANELS):
 
@@ -338,12 +348,11 @@
         y_copy(half).start()
     run_filter(3)
     y_copy(3).start()
-    inner(3, bulk, 128)
+    send_halo(6)
     gram.over_x()
-    run_filter(4)
-    y_copy(4).start()
-    inner(4, bulk, 192)
+    send_halo(7)
     gram.end()
+    send_halo(8)
 
     g = gram.full[...]
     eye = identity(PANEL)
@@ -354,33 +363,30 @@
     a = a - exact(exact_t(g[PANEL:], t0), t0)
     ag = exact(a, g)
     s1 = exact_t(ag[:PANEL], a[:PANEL])
-    run_filter(5)
-    y_copy(5).start()
-    inner(5, bulk, 224)
+    for c in (4, 5, 6, 7):
+        run_filter(c)
+        y_copy(c).start()
+    inner(128, 128, bulk, 128)
     bulk.start()
     t1 = exact(inv_sqrt(s1), a[:PANEL])
     t1g = exact(t1, g)
+    bulk.over_z()
     a = a[PANEL:] - exact(exact_t(ag[PANEL:], t1), t1)
     s2 = exact_t(exact(a, g), a)
-    bulk.over_z()
-    run_filter(6)
-    y_copy(6).start()
-    inner(6, last, 0)
-    run_filter(7)
-    y_copy(7).start()
-    inner(7, last, 32)
+    for c in (8,):
+        run_filter(c)
+        y_copy(c).start()
+    inner(BULK, ROWS - BULK, last, 0)
     last.start()
-    t2 = exact(inv_sqrt(s2), a)
-    bulk.over_x()
-    last.over_z()
+    t2 = exact(inv_sqrt(s2, (bulk.over_x, last.over_z)), a)
+    bulk.end()
+    last.over_x()
     t2g = exact(t2, g)
     r0 = t0
     r1 = t1 - exact(exact_t(t1g, t0), r0)
     r2 = t2 - exact(exact_t(t2g, t0), r0) - exact(exact_t(t2g, t1), r1)
     t = jnp.concatenate([t0, t1, t2], axis=0)
     r = jnp.concatenate([r0, r1, r2], axis=0)
-    bulk.end()
-    last.over_x()
     d_out[:BULK] = exact(exact_t(bulk.full[...], r), t)
     for p, rows in enumerate((t0, t1, t2)):
 
@@ -428,7 +434,7 @@
         pltpu.SemaphoreType.DMA((PANELS, 2)),
         pltpu.SemaphoreType.DMA((3 + len(CHUNKS),)),
     ]
-    anywhere = pl.BlockSpec(memory_space=pl.ANY)
+    anywhere = pl.BlockSpec(memory_space=pltpu.HBM)
     return pl.pallas_call(
         body,
         out_shape=(
@@ -444,7 +450,7 @@
     )(orb, pot)
 
 
-STEP = 64
+STEP = 160
 
 
 def update_body(y, p, d, out, ph, plo):
@@ -465,7 +471,7 @@
             flat[pl.ds(i * 128 + k, 8, stride=16), :] = rows[i * 8 : i * 8 + 8]
         return 0
 
-    lax.fori_loop(0, 16, some, 0)
+    lax.fori_loop(0, 16, some, 0, unroll=4)
 
 
 def update(y, p, d):

time: 159 us -> 110 us (0.69)
  Pallas kernels: 156 us -> 108 us
    pallas_call x1, Pallas kernels: 139 us -> 103 us  [project(): pl.pallas_call(body, out_shape=(jax.ShapeDtypeStruct((16, ROWS, 128), F32...]
    pallas_call x1, Pallas kernels: 16.9 us -> 5.08 us  [update(): pl.pallas_call(update_body, grid=(ROWS // STEP,), out_shape=jax.ShapeDtyp...]
where the time goes in v2:
time: 110 us
  Pallas kernels  108 us (98%)
  local copies, waits for them, and re-layouts  2.44 us (2%)
    pallas_call x1, Pallas kernels, project(): pl.pallas_call(body, out_shape=(jax.ShapeDtypeStruct((16, ROWS, 128), F32...  103 us
    pallas_call x1, Pallas kernels, update(): pl.pallas_call(update_body, grid=(ROWS // STEP,), out_shape=jax.ShapeDtyp...  5.08 us
    unnamed x4, local copies, waits for them, and re-layouts  2.44 us

profile of v2, /device:TPU:16, one launch (start us, length us, event | category | flops | bytes accessed | tf_op | source)
XLA Modules:
  0.0 110.3 jit_solution(430999137949098837)
XLA Ops:
  0.0 0.0 copy-start
  0.0 1.7 %copy-done = f32[320,2,8,128]{3,2,1,0:T(8,128)S(1)} copy-done((f32[320,2,8,128]{3,2,1,0:T(8,128)S(1)}, f32[320,2,8,128]{3,2,1,0:T(8,128)}, u32[]{:S(2)}) %copy-start) | copy-done | bytes 2621464
  1.7 0.0 copy-start.1
  1.7 0.7 copy-done.1
  2.4 102.8 %filter_and_project.1 = (f32[16,320,128]{2,1,0:T(8,128)S(1)}, f32[16,192,128]{2,1,0:T(8,128)S(1)}, f32[320,192]{1,0:T(8,128)S(1)}) custom-call(f32[320,2,8,128]{3,2,1,0:T(8,128)S(1)} %copy-done, f32[2,8,128]{2,1,0:T(8,128)S(1)} %copy-done.1), custom_call_target="tpu_custom_call" | custom-call | tf_op jit(solution)/shard_map/filter_and_project/pallas_call | solution.py:438
  105.2 5.1 %apply_update.1 = f32[320,2,8,128]{3,2,1,0:T(8,128)} custom-call(f32[16,320,128]{2,1,0:T(8,128)S(1)} %get-tuple-element.8.y, f32[16,192,128]{2,1,0:T(8,128)S(1)} %get-tuple-element.9.p, f32[320,192]{1,0:T(8,128)S(1)} %get-tuple-element.10.d), custom_call_target="tpu_custom_call" | custom-call | tf_op jit(solution)/shard_map/apply_update/pallas_call | solution.py:478
Async XLA Ops:
  0.0 1.7 %copy-start = (f32[320,2,8,128]{3,2,1,0:T(8,128)S(1)}, f32[320,2,8,128]{3,2,1,0:T(8,128)}, u32[]{:S(2)}) copy-start(f32[320,2,8,128]{3,2,1,0:T(8,128)} %orb.1) | copy-start | bytes 7864324
  1.7 0.7 copy-start.1

commit v3 on v2

--- a/solution.py
+++ b/solution.py
@@ -223,6 +223,14 @@
         for copy in halo(c):
             copy.start()
 
+    def send_inside(c):
+        for copy, edge in zip(halo(c), (3, 0)):
+            pl.when(gram.x != edge)(copy.start)
+
+    def send_around(c):
+        for copy, edge in zip(halo(c), (3, 0)):
+            pl.when(gram.x == edge)(copy.start)
+
     def pot_halo():
         return [
             remote(pot, pots.at[0], pot_s.at[0], pot_r.at[0], {"dom": right}),
@@ -334,7 +342,7 @@
     send_halo(4)
     inner(0, 128, bulk, 0)
     gram.over_z()
-    send_halo(5)
+    send_inside(5)
     for half in range(2):
         for p in range(PANELS):
 
@@ -348,17 +356,20 @@
         y_copy(half).start()
     run_filter(3)
     y_copy(3).start()
-    send_halo(6)
+    send_inside(6)
     gram.over_x()
-    send_halo(7)
+    send_inside(7)
+    send_inside(8)
     gram.end()
-    send_halo(8)
+    send_around(5)
+    send_around(6)
+    send_around(7)
+    send_around(8)
 
     g = gram.full[...]
     eye = identity(PANEL)
     none = jnp.zeros((PANEL, PANEL), F32)
     t0 = jnp.concatenate([inv_sqrt(g[:PANEL, :PANEL]), none, none], axis=1)
-    t0g = exact(t0, g)
     a = jnp.concatenate([jnp.concatenate([none, eye, none], axis=1), jnp.concatenate([none, none, eye], axis=1)], axis=0)
     a = a - exact(exact_t(g[PANEL:], t0), t0)
     ag = exact(a, g)
@@ -368,25 +379,26 @@
         y_copy(c).start()
     inner(128, 128, bulk, 128)
     bulk.start()
-    t1 = exact(inv_sqrt(s1), a[:PANEL])
-    t1g = exact(t1, g)
+    root1 = inv_sqrt(s1)
+    t1 = exact(root1, a[:PANEL])
+    r1 = t1 - exact(exact_t(exact(root1, ag[:PANEL]), t0), t0)
+    t01 = jnp.concatenate([t0, t1], axis=0)
+    r01 = jnp.concatenate([t0, r1], axis=0)
     bulk.over_z()
-    a = a[PANEL:] - exact(exact_t(ag[PANEL:], t1), t1)
-    s2 = exact_t(exact(a, g), a)
+    a2 = a[PANEL:] - exact(exact_t(ag[PANEL:], t1), t1)
+    a2g = exact(a2, g)
+    s2 = exact_t(a2g, a2)
     for c in (8,):
         run_filter(c)
         y_copy(c).start()
     inner(BULK, ROWS - BULK, last, 0)
     last.start()
-    t2 = exact(inv_sqrt(s2, (bulk.over_x, last.over_z)), a)
+    root2 = inv_sqrt(s2, (bulk.over_x, last.over_z, last.over_x))
+    t2 = exact(root2, a2)
+    before = exact_t(exact(root2, a2g), t01)
     bulk.end()
-    last.over_x()
-    t2g = exact(t2, g)
-    r0 = t0
-    r1 = t1 - exact(exact_t(t1g, t0), r0)
-    r2 = t2 - exact(exact_t(t2g, t0), r0) - exact(exact_t(t2g, t1), r1)
-    t = jnp.concatenate([t0, t1, t2], axis=0)
-    r = jnp.concatenate([r0, r1, r2], axis=0)
+    t = jnp.concatenate([t01, t2], axis=0)
+    r = jnp.concatenate([r01, t2 - exact(before, r01)], axis=0)
     d_out[:BULK] = exact(exact_t(bulk.full[...], r), t)
     for p, rows in enumerate((t0, t1, t2)):
 
@@ -471,7 +483,7 @@
             flat[pl.ds(i * 128 + k, 8, stride=16), :] = rows[i * 8 : i * 8 + 8]
         return 0
 
-    lax.fori_loop(0, 16, some, 0, unroll=4)
+    lax.fori_loop(0, 16, some, 0, unroll=8)
 
 
 def update(y, p, d):

time: 110 us -> 109 us (level)
  Pallas kernels: 108 us -> 106 us
    pallas_call x1, Pallas kernels: 103 us -> 102 us  [project(): pl.pallas_call(body, out_shape=(jax.ShapeDtypeStruct((16, ROWS, 128), F32...]
where the time goes in v3:
time: 109 us; the launch traced here: 108 us
  Pallas kernels  106 us (97%)
  local copies, waits for them, and re-layouts  2.44 us (2%)
    pallas_call x1, Pallas kernels, project(): pl.pallas_call(body, out_shape=(jax.ShapeDtypeStruct((16, ROWS, 128), F32...  102 us
    pallas_call x1, Pallas kernels, update(): pl.pallas_call(update_body, grid=(ROWS // STEP,), out_shape=jax.ShapeDtyp...  4.36 us
    unnamed x4, local copies, waits for them, and re-layouts  2.44 us

profile of v3, /device:TPU:16, one launch (start us, length us, event | category | flops | bytes accessed | tf_op | source)
XLA Modules:
  0.0 108.3 jit_solution(14174051087260269538)
XLA Ops:
  0.0 0.0 copy-start
  0.0 1.7 %copy-done = f32[320,2,8,128]{3,2,1,0:T(8,128)S(1)} copy-done((f32[320,2,8,128]{3,2,1,0:T(8,128)S(1)}, f32[320,2,8,128]{3,2,1,0:T(8,128)}, u32[]{:S(2)}) %copy-start) | copy-done | bytes 2621464
  1.7 0.0 copy-start.1
  1.7 0.7 copy-done.1
  2.4 101.5 %filter_and_project.1 = (f32[16,320,128]{2,1,0:T(8,128)S(1)}, f32[16,192,128]{2,1,0:T(8,128)S(1)}, f32[320,192]{1,0:T(8,128)S(1)}) custom-call(f32[320,2,8,128]{3,2,1,0:T(8,128)S(1)} %copy-done, f32[2,8,128]{2,1,0:T(8,128)S(1)} %copy-done.1), custom_call_target="tpu_custom_call" | custom-call | tf_op jit(solution)/shard_map/filter_and_project/pallas_call | solution.py:450
  104.0 4.4 %apply_update.1 = f32[320,2,8,128]{3,2,1,0:T(8,128)} custom-call(f32[16,320,128]{2,1,0:T(8,128)S(1)} %get-tuple-element.8.y, f32[16,192,128]{2,1,0:T(8,128)S(1)} %get-tuple-element.9.p, f32[320,192]{1,0:T(8,128)S(1)} %get-tuple-element.10.d), custom_call_target="tpu_custom_call" | custom-call | tf_op jit(solution)/shard_map/apply_update/pallas_call | solution.py:490
Async XLA Ops:
  0.0 1.7 %copy-start = (f32[320,2,8,128]{3,2,1,0:T(8,128)S(1)}, f32[320,2,8,128]{3,2,1,0:T(8,128)}, u32[]{:S(2)}) copy-start(f32[320,2,8,128]{3,2,1,0:T(8,128)} %orb.1) | copy-start | bytes 7864324
  1.7 0.7 copy-start.1

commit v4 on v3

--- a/solution.py
+++ b/solution.py
@@ -317,7 +317,7 @@
             both = mm_t(jnp.concatenate([a0, a1], axis=1), jnp.concatenate([b0, b0], axis=1))
             return acc + (both + mm_t(a0, b1))
 
-        total.loc[at : at + count] = lax.fori_loop(0, 16, some, jnp.zeros((count, ALL), F32), unroll=4)
+        total.loc[at : at + count] = lax.fori_loop(0, 16, some, jnp.zeros((count, ALL), F32), unroll=16)
 
     run_filter(0)
     send_panel(0)
@@ -337,7 +337,7 @@
         plo[k] = a1
         return acc + (mm_t(a0, a0) + (mm_t(a0, a1) + mm_t(a1, a0)))
 
-    gram.loc[...] = lax.fori_loop(0, 16, gram_step, jnp.zeros((ALL, ALL), F32), unroll=4)
+    gram.loc[...] = lax.fori_loop(0, 16, gram_step, jnp.zeros((ALL, ALL), F32), unroll=8)
     gram.start()
     send_halo(4)
     inner(0, 128, bulk, 0)

time: 109 us -> 108 us (level)
  no operation moved by 1% of the time
where the time goes in v4:
time: 108 us
  Pallas kernels  105 us (97%)
  local copies, waits for them, and re-layouts  2.44 us (2%)
    pallas_call x1, Pallas kernels, project(): pl.pallas_call(body, out_shape=(jax.ShapeDtypeStruct((16, ROWS, 128), F32...  101 us
    pallas_call x1, Pallas kernels, update(): pl.pallas_call(update_body, grid=(ROWS // STEP,), out_shape=jax.ShapeDtyp...  4.36 us
    unnamed x4, local copies, waits for them, and re-layouts  2.44 us

profile of v4, /device:TPU:16, one launch (start us, length us, event | category | flops | bytes accessed | tf_op | source)
XLA Modules:
  0.0 107.9 jit_solution(5447683993029894401)
XLA Ops:
  0.0 0.0 copy-start
  0.0 1.7 %copy-done = f32[320,2,8,128]{3,2,1,0:T(8,128)S(1)} copy-done((f32[320,2,8,128]{3,2,1,0:T(8,128)S(1)}, f32[320,2,8,128]{3,2,1,0:T(8,128)}, u32[]{:S(2)}) %copy-start) | copy-done | bytes 2621464
  1.7 0.0 copy-start.1
  1.7 0.7 copy-done.1
  2.4 101.1 %filter_and_project.1 = (f32[16,320,128]{2,1,0:T(8,128)S(1)}, f32[16,192,128]{2,1,0:T(8,128)S(1)}, f32[320,192]{1,0:T(8,128)S(1)}) custom-call(f32[320,2,8,128]{3,2,1,0:T(8,128)S(1)} %copy-done, f32[2,8,128]{2,1,0:T(8,128)S(1)} %copy-done.1), custom_call_target="tpu_custom_call" | custom-call | tf_op jit(solution)/shard_map/filter_and_project/pallas_call | solution.py:450
  103.6 4.4 %apply_update.1 = f32[320,2,8,128]{3,2,1,0:T(8,128)} custom-call(f32[16,320,128]{2,1,0:T(8,128)S(1)} %get-tuple-element.8.y, f32[16,192,128]{2,1,0:T(8,128)S(1)} %get-tuple-element.9.p, f32[320,192]{1,0:T(8,128)S(1)} %get-tuple-element.10.d), custom_call_target="tpu_custom_call" | custom-call | tf_op jit(solution)/shard_map/apply_update/pallas_call | solution.py:490
Async XLA Ops:
  0.0 1.7 %copy-start = (f32[320,2,8,128]{3,2,1,0:T(8,128)S(1)}, f32[320,2,8,128]{3,2,1,0:T(8,128)}, u32[]{:S(2)}) copy-start(f32[320,2,8,128]{3,2,1,0:T(8,128)} %orb.1) | copy-start | bytes 7864324
  1.7 0.7 copy-start.1
